TPU v7x, 256 devices: a whole 4x4x8 slice. The times are simulated.
256 devices in a mesh: row: 4 (over x), col: 64 (over y, z, core).
Axes of the slice: x: 4, y: 4, z: 8, core: 2. Of those that a mesh axis runs over, the one named last changes fastest.
Arguments:
- activations: bfloat16 [8, 256, 8192], P('row')
- out_grads: bfloat16 [8, 256, 28672], P('row', None, 'col')
- valid_len: int32 [8], P('row'), may hold values from 1 to 256, 1024 in all
- weight: bfloat16 [8192, 28672], P('row', 'col'), may hold values from -0.0625 to 0.0625
- sketch: bfloat16 [28672, 512], P('col'), may hold values from -6 to 6
Outputs:
- basis: float32 [8192, 512], P(('row', 'col'))
- coeffs: float32 [512, 28672], P('row', 'col')
Inputs may be any that keep to these rules, and one draw needn't show every extreme that they name: `valid_len`: valid tokens of each sequence; at least one sequence fills all 256 slots.
All inputs are finite; a program needn't handle non-finite values. No bound on the sum of `valid_len` on one device may be relied on, other than what follows from the above.
Results may differ from a plain program's by a relative error of at most 0.01.
Values may be sent and summed in bfloat16 or wider, within the bound.
A program may use at most 64 MiB of HBM per device.

v0:
```python
import math
import jax
import jax.numpy as jnp
from jax import lax
from jax.sharding import PartitionSpec as P


def contract_rows(left, right):
    return lax.dot_general(
        left, right, (((0,), (0,)), ((), ())), preferred_element_type=jnp.float32
    )


def gram_local(sketch_rows):
    return lax.dot_general(
        sketch_rows, sketch_rows, (((0,), (0,)), ((), ())), precision=lax.Precision.HIGHEST
    )


def solve_basis(gram, sketch_rows):
    factor_low = jnp.linalg.cholesky(gram)
    return lax.linalg.triangular_solve(
        factor_low, sketch_rows, left_side=False, lower=True, transpose_a=True
    )


def orthonormal_shared(sketch_rows):
    gram = lax.psum(gram_local(sketch_rows), ("row", "col"))
    return solve_basis(gram, sketch_rows)


def reduce_sketch(left, right):
    return lax.psum_scatter(
        jnp.dot(left, right, preferred_element_type=jnp.float32),
        "col",
        scatter_dimension=0,
        tiled=True,
    )


def local(activations, out_grads, valid_len, weight, sketch):
    seq_dev, length, model_width = activations.shape
    rows_here, cols_here = weight.shape
    col_count = lax.axis_size("col")
    col_index = lax.axis_index("col")
    row_index = lax.axis_index("row")
    own_rows = rows_here // col_count
    own_start = col_index * own_rows
    positions = lax.iota(jnp.int32, length)
    raw_sketch = reduce_sketch(weight, sketch)
    partial_mass = jnp.zeros((model_width,), jnp.float32)
    for seq_index in range(seq_dev):
        valid = (positions < valid_len[seq_index]).astype(jnp.bfloat16)
        grad_block = contract_rows(activations[seq_index], out_grads[seq_index] * valid[:, None])
        partial_mass = partial_mass + jnp.sum(grad_block * grad_block, axis=1)
    fisher = lax.psum(partial_mass, ("row", "col"))
    total_mass = jnp.sum(fisher)
    own_mass = lax.dynamic_slice_in_dim(fisher, row_index * rows_here, rows_here, 0)
    row_scale = jnp.sqrt(own_mass / (total_mass / model_width + 1e-06))
    first_sketch = (
        lax.dynamic_slice_in_dim(row_scale, own_start, own_rows, 0)[:, None] * raw_sketch
    ).astype(jnp.bfloat16)
    scaled = (row_scale[:, None] * weight.astype(jnp.float32)).astype(jnp.bfloat16)
    proj_part = contract_rows(scaled, lax.all_gather(first_sketch, "col", axis=0, tiled=True))
    projected = lax.psum(proj_part, "row").astype(jnp.bfloat16)
    second_sketch = reduce_sketch(scaled, projected)
    second_basis = orthonormal_shared(second_sketch)
    group_second = lax.all_gather(second_basis.astype(jnp.bfloat16), "col", axis=0, tiled=True)
    coeff_raw = lax.psum_scatter(
        contract_rows(group_second, scaled).astype(jnp.bfloat16),
        "row",
        scatter_dimension=0,
        tiled=True,
    ).astype(jnp.float32)
    return (second_basis * math.sqrt(model_width), coeff_raw * math.sqrt(cols_here * col_count))


def solution(mesh):
    placed = (
        P("row", None, None),
        P("row", None, "col"),
        P("row"),
        P("row", "col"),
        P("col", None),
    )
    return jax.shard_map(
        local,
        mesh=mesh,
        in_specs=placed,
        out_specs=(P(("row", "col"), None), P("row", "col")),
        check_vma=False,
    )
```

profile of v0, /device:TPU:8, one launch (start us, length us, event | category | flops | bytes accessed | tf_op | source)
XLA Modules:
  0.0 952.2 jit_solution(8031663152801272860)
XLA Ops:
  8.2 4.7 fusion.51
  15.5 4.3 multiply_reduce_fusion
  19.8 4.4 multiply_reduce_fusion.1
  24.2 78.7 %psum.21 = f32[8192]{0:T(1024)S(1)} all-reduce(f32[8192]{0:T(1024)S(1)} %add.64), channel_id=1, replica_groups=mesh['row'=4,'col'=64] {'row','col'}, use_global_device_ids=true, to_apply=%region_2.0 | all-reduce | flops 8192 | bytes 65536 | tf_op jit(solution)/shard_map/psum | solution.py:56
  104.3 55.4 %reduce-scatter.6.cloned.1.call-done = f32[32,512]{1,0:T(8,128)} async-done(((f32[2048,512]{1,0:T(8,128)}), f32[32,512]{1,0:T(8,128)}) %reduce-scatter.6.cloned.1.call-update) | async-done | bytes 65552 | tf_op jit(solution)/shard_map/reduce_scatter | solution.py:33
  159.7 1.5 multiply_convert_fusion.6
  161.3 77.5 %all-gather.3.cloned.1.call-done = bf16[2048,512]{1,0:T(8,128)(2,1)} async-done(((bf16[32,512]{1,0:T(8,128)(2,1)}), bf16[2048,512]{1,0:T(8,128)(2,1)}) %all-gather.3.cloned.1.call-update) | async-done | bytes 2097168 | tf_op jit(solution)/shard_map/all_gather | solution.py:64
  238.8 3.6 fusion.6
  242.5 27.8 %all-reduce.5 = bf16[448,512]{1,0:T(8,128)(2,1)S(1)} all-reduce(f32[448,512]{1,0:T(8,128)} %fusion.6), channel_id=1, replica_groups=mesh['row'=4,'col'=64] {'row'}, use_global_device_ids=true, to_apply=%region_5.0 | all-reduce | flops 229376 | bytes 1376256 | tf_op jit(solution)/shard_map/psum | solution.py:65
  270.2 3.2 fusion.5
  273.5 141.3 %reduce-scatter.8.cloned.1.call-done = f32[32,512]{1,0:T(8,128)} async-done(((f32[2048,512]{1,0:T(8,128)}), f32[32,512]{1,0:T(8,128)}) %reduce-scatter.8.cloned.1.call-update) | async-done | bytes 65552 | tf_op jit(solution)/shard_map/reduce_scatter | solution.py:33
  414.8 3.0 fusion.52
  418.8 259.1 %all-reduce.4.cloned.1.call-done = f32[512,512]{0,1:T(8,128)} async-done(((f32[512,512]{0,1:T(8,128)}), f32[512,512]{0,1:T(8,128)}) %all-reduce.4.cloned.1.call-update) | async-done | bytes 1048592 | tf_op jit(solution)/shard_map/psum | solution.py:28
  677.9 1.6 copy.10
  682.0 11.7 %cholesky.104 = f32[128,128]{1,0:T(8,128)S(1)} custom-call(f32[128,128]{1,0:T(8,128)S(1)} %cholesky.266), custom_call_target="Cholesky" | custom-call | tf_op jit(solution)/shard_map/jit(cholesky)/cholesky | solution.py:21
  693.8 9.8 %custom-call.30 = f32[1,128,128]{1,2,0:T(8,128)S(1)} custom-call(f32[1,128,128]{2,1,0:T(8,128)S(1)} %get-tuple-element.29), custom_call_target="InvertDiagBlocksLowerTriangular" | custom-call | tf_op jit(solution)/shard_map/jit(cholesky)/cholesky | solution.py:21
  706.8 13.2 %cholesky.217 = f32[128,128]{1,0:T(8,128)} custom-call(f32[128,128]{1,0:T(8,128)} %cholesky.270), custom_call_target="Cholesky" | custom-call | tf_op jit(solution)/shard_map/jit(cholesky)/cholesky | solution.py:21
  720.0 1.5 select_reduce_fusion.2
  721.5 11.4 %custom-call.31 = f32[1,128,128]{1,2,0:T(8,128)} custom-call(f32[1,128,128]{2,1,0:T(8,128)} %get-tuple-element.26), custom_call_target="InvertDiagBlocksLowerTriangular" | custom-call | tf_op jit(solution)/shard_map/jit(cholesky)/cholesky | solution.py:21
  735.9 13.2 %cholesky.238 = f32[128,128]{1,0:T(8,128)} custom-call(f32[128,128]{1,0:T(8,128)} %cholesky.275), custom_call_target="Cholesky" | custom-call | tf_op jit(solution)/shard_map/jit(cholesky)/cholesky | solution.py:21
  749.1 1.5 select_reduce_fusion.1
  751.3 11.3 %custom-call.32 = f32[1,128,128]{1,2,0:T(8,128)} custom-call(f32[1,128,128]{2,1,0:T(8,128)} %get-tuple-element.23), custom_call_target="InvertDiagBlocksLowerTriangular" | custom-call | tf_op jit(solution)/shard_map/jit(cholesky)/cholesky | solution.py:21
  764.9 11.7 %cholesky.255 = f32[128,128]{1,0:T(8,128)S(1)} custom-call(f32[128,128]{1,0:T(8,128)S(1)} %convolution_subtract_fusion.2), custom_call_target="Cholesky" | custom-call | tf_op jit(solution)/shard_map/jit(cholesky)/cholesky | solution.py:21
  782.4 14.0 %while.1 = (s32[]{:T(128)}, f32[512,512]{1,0:T(8,128)}, s32[4,2]{0,1:T(2,128)S(1)}, f32[4,128,128]{2,1,0:T(8,128)}, s32[]{:T(128)}) while((s32[]{:T(128)}, f32[512,512]{1,0:T(8,128)}, s32[4,2]{0,1:T(2,128)S(1)}, f32[4,128,128]{2,1,0:T(8,128)}, s32[]{:T(128)}) %tuple.32), condition=%wide.while_cond, body=%wide.while_body.sunk | while | flops 2 | bytes 132705 | solution.py:22
  783.0 2.9 bitcast_dynamic-update-slice_fusion.2
  786.5 2.9 bitcast_dynamic-update-slice_fusion.2
  790.0 2.9 bitcast_dynamic-update-slice_fusion.2
  793.5 2.8 bitcast_dynamic-update-slice_fusion.2
  796.3 40.1 %custom-call.33 = f32[4,128,128]{1,2,0:T(8,128)S(1)} custom-call(f32[4,128,128]{2,1,0:T(8,128)} %get-tuple-element.9), custom_call_target="InvertDiagBlocksLowerTriangular" | custom-call | tf_op jit(solution)/shard_map/triangular_solve | solution.py:22
  841.4 75.5 %all-gather.5.cloned.1.call-done = bf16[2048,512]{1,0:T(8,128)(2,1)} async-done(((bf16[32,512]{1,0:T(8,128)(2,1)}), bf16[2048,512]{1,0:T(8,128)(2,1)}) %all-gather.5.cloned.1.call-update) | async-done | bytes 2097168 | tf_op jit(solution)/shard_map/all_gather | solution.py:68
  916.8 2.7 fusion.7
  921.2 22.2 %reduce-scatter.10.cloned.1.call-done = bf16[128,448]{1,0:T(8,128)(2,1)} async-done(((bf16[512,448]{1,0:T(8,128)(2,1)}), bf16[128,448]{1,0:T(8,128)(2,1)}) %reduce-scatter.10.cloned.1.call-update) | async-done | bytes 114704
  (71 shorter events, 30.9 us)
Async XLA Ops:
  7.2 1.0 copy-start
  7.2 152.5 %reduce-scatter.6.cloned.1.call-start = ((), (), s32[]{:S(2)}) async-start(), calls=%async_computation.3 | async-start | bytes 4259840 | tf_op jit(solution)/shard_map/reduce_scatter | solution.py:33
  12.9 0.7 copy-start.4
  12.9 2.6 copy-start.5
  12.9 225.9 %all-gather.3.cloned.1.call-start = ((), (), s32[]{:S(2)}) async-start(), calls=%async_computation.4 | async-start | bytes 2129920 | tf_op jit(solution)/shard_map/all_gather | solution.py:64
  19.8 219.0 %copy-start.1 = (bf16[2048,448]{0,1:T(8,128)(2,1)S(1)}, bf16[2048,448]{0,1:T(8,128)(2,1)}, u32[]{:S(2)}) copy-start(bf16[2048,448]{0,1:T(8,128)(2,1)} %param.8) | copy-start | bytes 5505028
  161.3 253.6 %reduce-scatter.8.cloned.1.call-start = ((), (), s32[]{:S(2)}) async-start(), calls=%async_computation.5 | async-start | bytes 4259840 | tf_op jit(solution)/shard_map/reduce_scatter | solution.py:33
  273.5 404.4 %all-reduce.4.cloned.1.call-start = ((), (), s32[]{:S(2)}) async-start(), calls=%async_computation.6 | async-start | bytes 2097152 | tf_op jit(solution)/shard_map/psum | solution.py:28
  417.8 499.0 %all-gather.5.cloned.1.call-start = ((), (), s32[]{:S(2)}) async-start(), calls=%async_computation.7 | async-start | bytes 2129920 | tf_op jit(solution)/shard_map/all_gather | solution.py:68
  680.9 1.0 copy-start.2
  734.0 102.5 %copy-start.3 = (f32[32,512]{1,0:T(8,128)S(1)}, f32[32,512]{1,0:T(8,128)}, u32[]{:S(2)}) copy-start(f32[32,512]{1,0:T(8,128)} %reduce-scatter.8.cloned.1.call-done) | copy-start | bytes 196612
  841.3 102.1 %reduce-scatter.10.cloned.1.call-start = ((), (), s32[]{:S(2)}) async-start(), calls=%async_computation.8 | async-start | bytes 655360
Sparse Core Ops, SparseCore 0:
  13.1 146.6 reduce-scatter.5
  163.1 75.7 all-gather.2
  273.6 141.1 reduce-scatter.7
  420.1 257.7 all-reduce.3
  841.4 75.3 all-gather.4
  920.7 22.6 reduce-scatter.9
where the time goes:
time: 961 us; the launch traced here: 952 us
  waiting for transfers between devices  631 us (66%)
  other arithmetic  136 us (14%)
  blocking collectives  106 us (11%)
  matrix products  37.2 us (4%)
  local copies, waits for them, and re-layouts  22.7 us (2%)
  between operations  17.8 us (2%)
    psum x1, waiting for transfers between devices, orthonormal_shared(): gram = lax.psum(gram_local(sketch_rows), ('row', 'col'))  259 us
    reduce_scatter x2, waiting for transfers between devices, reduce_sketch(): lax.psum_scatter(jnp.dot(left, right, preferred_element_type=jnp.float32)...  197 us
    another operation x14, other arithmetic, solve_basis(): factor_low = jnp.linalg.cholesky(gram)  87.3 us
    psum x1, blocking collectives, local(): fisher = lax.psum(partial_mass, ('row', 'col'))  78.7 us
    all_gather x1, waiting for transfers between devices, local(): lax.all_gather(first_sketch, 'col', axis=0, tiled=True)  77.5 us
    all_gather x1, waiting for transfers between devices, local(): lax.all_gather(second_basis.astype(jnp.bfloat16), 'col', axis=0, tiled=True)  75.5 us
    another operation x3, other arithmetic, solve_basis(): lax.linalg.triangular_solve(factor_low, sketch_rows, left_side=False, low...  42 us
    psum x1, blocking collectives, local(): projected = lax.psum(proj_part, 'row').astype(jnp.bfloat16)  27.8 us
  transfers between devices with their start and end apart: 6, of which 6 were waited for; matrix products, arithmetic and copies ran while one was open for 1% of the time, Pallas kernels for 0%

commit v1 on v0

--- a/solution.py
+++ b/solution.py
@@ -25,7 +25,8 @@
 
 
 def orthonormal_shared(sketch_rows):
-    gram = lax.psum(gram_local(sketch_rows), ("row", "col"))
+    partial = lax.psum(gram_local(sketch_rows), "row")
+    gram = lax.psum(partial, "col")
     return solve_basis(gram, sketch_rows)
 
 

time: 961 us -> 941 us (0.979)
  waiting for transfers between devices: 631 us -> 611 us
    psum x1 -> x2, waiting for transfers between devices: 259 us -> 240 us  [the longest x1 190 us: orthonormal_shared(): gram = lax.psum(partial, 'col')]
    unnamed x7 -> x8, waiting for transfers between devices: 22.3 us -> 22.4 us
  transfers between devices with their start and end apart: 6 -> 7, of which waited for: 6 -> 7; matrix products, arithmetic and copies ran while one was open for 1% -> 1% of each run, Pallas kernels for 0% -> 0%
where the time goes in v1:
time: 941 us; the launch traced here: 932 us
  waiting for transfers between devices  611 us (65%)
  other arithmetic  136 us (14%)
  blocking collectives  106 us (11%)
  matrix products  37.2 us (4%)
  local copies, waits for them, and re-layouts  22.7 us (2%)
  between operations  17.8 us (2%)
    reduce_scatter x2, waiting for transfers between devices, reduce_sketch(): lax.psum_scatter(jnp.dot(left, right, preferred_element_type=jnp.float32)...  197 us
    psum x1, waiting for transfers between devices, orthonormal_shared(): gram = lax.psum(partial, 'col')  190 us
    another operation x14, other arithmetic, solve_basis(): factor_low = jnp.linalg.cholesky(gram)  87.3 us
    psum x1, blocking collectives, local(): fisher = lax.psum(partial_mass, ('row', 'col'))  78.7 us
    all_gather x1, waiting for transfers between devices, local(): lax.all_gather(first_sketch, 'col', axis=0, tiled=True)  77.5 us
    all_gather x1, waiting for transfers between devices, local(): lax.all_gather(second_basis.astype(jnp.bfloat16), 'col', axis=0, tiled=True)  73.8 us
    psum x1, waiting for transfers between devices, orthonormal_shared(): partial = lax.psum(gram_local(sketch_rows), 'row')  50.4 us
    another operation x3, other arithmetic, solve_basis(): lax.linalg.triangular_solve(factor_low, sketch_rows, left_side=False, low...  42 us
  transfers between devices with their start and end apart: 7, of which 7 were waited for; matrix products, arithmetic and copies ran while one was open for 1% of the time, Pallas kernels for 0%

profile of v1, /device:TPU:8, one launch (start us, length us, event | category | flops | bytes accessed | tf_op | source)
XLA Modules:
  0.0 931.9 jit_solution(876508169969290248)
XLA Ops:
  8.2 4.7 fusion.51
  15.5 4.3 multiply_reduce_fusion
  19.8 4.4 multiply_reduce_fusion.1
  24.2 78.7 %psum.28 = f32[8192]{0:T(1024)S(1)} all-reduce(f32[8192]{0:T(1024)S(1)} %add.66), channel_id=1, replica_groups=mesh['row'=4,'col'=64] {'row','col'}, use_global_device_ids=true, to_apply=%region_2.0 | all-reduce | flops 8192 | bytes 65536 | tf_op jit(solution)/shard_map/psum | solution.py:57
  104.3 55.4 %reduce-scatter.6.cloned.1.call-done = f32[32,512]{1,0:T(8,128)} async-done(((f32[2048,512]{1,0:T(8,128)}), f32[32,512]{1,0:T(8,128)}) %reduce-scatter.6.cloned.1.call-update) | async-done | bytes 65552 | tf_op jit(solution)/shard_map/reduce_scatter | solution.py:34
  159.7 1.5 multiply_convert_fusion.6
  161.3 77.5 %all-gather.3.cloned.1.call-done = bf16[2048,512]{1,0:T(8,128)(2,1)} async-done(((bf16[32,512]{1,0:T(8,128)(2,1)}), bf16[2048,512]{1,0:T(8,128)(2,1)}) %all-gather.3.cloned.1.call-update) | async-done | bytes 2097168 | tf_op jit(solution)/shard_map/all_gather | solution.py:65
  238.8 3.6 fusion.6
  242.5 27.8 %all-reduce.8 = bf16[448,512]{1,0:T(8,128)(2,1)S(1)} all-reduce(f32[448,512]{1,0:T(8,128)} %fusion.6), channel_id=1, replica_groups=mesh['row'=4,'col'=64] {'row'}, use_global_device_ids=true, to_apply=%region_5.0 | all-reduce | flops 229376 | bytes 1376256 | tf_op jit(solution)/shard_map/psum | solution.py:66
  270.2 3.2 fusion.5
  273.5 141.3 %reduce-scatter.8.cloned.1.call-done = f32[32,512]{1,0:T(8,128)} async-done(((f32[2048,512]{1,0:T(8,128)}), f32[32,512]{1,0:T(8,128)}) %reduce-scatter.8.cloned.1.call-update) | async-done | bytes 65552 | tf_op jit(solution)/shard_map/reduce_scatter | solution.py:34
  414.8 3.0 fusion.52
  417.9 50.4 %all-reduce.5.cloned.1.call-done = f32[512,512]{0,1:T(8,128)} async-done(((f32[512,512]{0,1:T(8,128)}), f32[512,512]{0,1:T(8,128)}) %all-reduce.5.cloned.1.call-update) | async-done | bytes 1048592 | tf_op jit(solution)/shard_map/psum | solution.py:28
  469.3 190.0 %all-reduce.7.cloned.1.call-done = f32[512,512]{0,1:T(8,128)} async-done(((f32[512,512]{0,1:T(8,128)}), f32[512,512]{0,1:T(8,128)}) %all-reduce.7.cloned.1.call-update) | async-done | bytes 1048592 | tf_op jit(solution)/shard_map/psum | solution.py:29
  659.3 1.6 copy.10
  663.3 11.7 %cholesky.104 = f32[128,128]{1,0:T(8,128)S(1)} custom-call(f32[128,128]{1,0:T(8,128)S(1)} %cholesky.266), custom_call_target="Cholesky" | custom-call | tf_op jit(solution)/shard_map/jit(cholesky)/cholesky | solution.py:21
  675.2 9.8 %custom-call.30 = f32[1,128,128]{1,2,0:T(8,128)S(1)} custom-call(f32[1,128,128]{2,1,0:T(8,128)S(1)} %get-tuple-element.29), custom_call_target="InvertDiagBlocksLowerTriangular" | custom-call | tf_op jit(solution)/shard_map/jit(cholesky)/cholesky | solution.py:21
  688.1 13.2 %cholesky.217 = f32[128,128]{1,0:T(8,128)} custom-call(f32[128,128]{1,0:T(8,128)} %cholesky.270), custom_call_target="Cholesky" | custom-call | tf_op jit(solution)/shard_map/jit(cholesky)/cholesky | solution.py:21
  701.3 1.5 select_reduce_fusion.2
  702.8 11.4 %custom-call.31 = f32[1,128,128]{1,2,0:T(8,128)} custom-call(f32[1,128,128]{2,1,0:T(8,128)} %get-tuple-element.26), custom_call_target="InvertDiagBlocksLowerTriangular" | custom-call | tf_op jit(solution)/shard_map/jit(cholesky)/cholesky | solution.py:21
  717.3 13.2 %cholesky.238 = f32[128,128]{1,0:T(8,128)} custom-call(f32[128,128]{1,0:T(8,128)} %cholesky.275), custom_call_target="Cholesky" | custom-call | tf_op jit(solution)/shard_map/jit(cholesky)/cholesky | solution.py:21
  732.7 11.3 %custom-call.32 = f32[1,128,128]{1,2,0:T(8,128)} custom-call(f32[1,128,128]{2,1,0:T(8,128)} %get-tuple-element.23), custom_call_target="InvertDiagBlocksLowerTriangular" | custom-call | tf_op jit(solution)/shard_map/jit(cholesky)/cholesky | solution.py:21
  746.2 11.7 %cholesky.255 = f32[128,128]{1,0:T(8,128)S(1)} custom-call(f32[128,128]{1,0:T(8,128)S(1)} %convolution_subtract_fusion.2), custom_call_target="Cholesky" | custom-call | tf_op jit(solution)/shard_map/jit(cholesky)/cholesky | solution.py:21
  763.7 14.0 %while.1 = (s32[]{:T(128)}, f32[512,512]{1,0:T(8,128)}, s32[4,2]{0,1:T(2,128)S(1)}, f32[4,128,128]{2,1,0:T(8,128)}, s32[]{:T(128)}) while((s32[]{:T(128)}, f32[512,512]{1,0:T(8,128)}, s32[4,2]{0,1:T(2,128)S(1)}, f32[4,128,128]{2,1,0:T(8,128)}, s32[]{:T(128)}) %tuple.32), condition=%wide.while_cond, body=%wide.while_body.sunk | while | flops 2 | bytes 132705 | solution.py:22
  764.3 2.9 bitcast_dynamic-update-slice_fusion.2
  767.8 2.9 bitcast_dynamic-update-slice_fusion.2
  771.4 2.9 bitcast_dynamic-update-slice_fusion.2
  774.9 2.8 bitcast_dynamic-update-slice_fusion.2
  777.7 40.1 %custom-call.33 = f32[4,128,128]{1,2,0:T(8,128)S(1)} custom-call(f32[4,128,128]{2,1,0:T(8,128)} %get-tuple-element.9), custom_call_target="InvertDiagBlocksLowerTriangular" | custom-call | tf_op jit(solution)/shard_map/triangular_solve | solution.py:22
  822.7 73.8 %all-gather.5.cloned.1.call-done = bf16[2048,512]{1,0:T(8,128)(2,1)} async-done(((bf16[32,512]{1,0:T(8,128)(2,1)}), bf16[2048,512]{1,0:T(8,128)(2,1)}) %all-gather.5.cloned.1.call-update) | async-done | bytes 2097168 | tf_op jit(solution)/shard_map/all_gather | solution.py:69
  896.5 2.7 fusion.7
  900.8 22.3 %reduce-scatter.10.cloned.1.call-done = bf16[128,448]{1,0:T(8,128)(2,1)} async-done(((bf16[512,448]{1,0:T(8,128)(2,1)}), bf16[128,448]{1,0:T(8,128)(2,1)}) %reduce-scatter.10.cloned.1.call-update) | async-done | bytes 114704
  (74 shorter events, 32.5 us)
Async XLA Ops:
  7.2 1.0 copy-start
  7.2 152.5 %reduce-scatter.6.cloned.1.call-start = ((), (), s32[]{:S(2)}) async-start(), calls=%async_computation.3 | async-start | bytes 4259840 | tf_op jit(solution)/shard_map/reduce_scatter | solution.py:34
  12.9 0.7 copy-start.4
  12.9 2.6 copy-start.5
  12.9 225.9 %all-gather.3.cloned.1.call-start = ((), (), s32[]{:S(2)}) async-start(), calls=%async_computation.4 | async-start | bytes 2129920 | tf_op jit(solution)/shard_map/all_gather | solution.py:65
  19.8 219.0 %copy-start.1 = (bf16[2048,448]{0,1:T(8,128)(2,1)S(1)}, bf16[2048,448]{0,1:T(8,128)(2,1)}, u32[]{:S(2)}) copy-start(bf16[2048,448]{0,1:T(8,128)(2,1)} %param.8) | copy-start | bytes 5505028
  161.3 253.6 %reduce-scatter.8.cloned.1.call-start = ((), (), s32[]{:S(2)}) async-start(), calls=%async_computation.5 | async-start | bytes 4259840 | tf_op jit(solution)/shard_map/reduce_scatter | solution.py:34
  273.5 194.7 %all-reduce.5.cloned.1.call-start = ((), (), s32[]{:S(2)}) async-start(), calls=%async_computation.6 | async-start | bytes 2097152 | tf_op jit(solution)/shard_map/psum | solution.py:28
  417.8 241.5 %all-reduce.7.cloned.1.call-start = ((), (), s32[]{:S(2)}) async-start(), calls=%async_computation.7 | async-start | bytes 2097152 | tf_op jit(solution)/shard_map/psum | solution.py:29
  468.2 428.2 %all-gather.5.cloned.1.call-start = ((), (), s32[]{:S(2)}) async-start(), calls=%async_computation.8 | async-start | bytes 2129920 | tf_op jit(solution)/shard_map/all_gather | solution.py:69
  662.3 1.0 copy-start.2
  715.3 102.5 %copy-start.3 = (f32[32,512]{1,0:T(8,128)S(1)}, f32[32,512]{1,0:T(8,128)}, u32[]{:S(2)}) copy-start(f32[32,512]{1,0:T(8,128)} %reduce-scatter.8.cloned.1.call-done) | copy-start | bytes 196612
  822.7 100.4 %reduce-scatter.10.cloned.1.call-start = ((), (), s32[]{:S(2)}) async-start(), calls=%async_computation.9 | async-start | bytes 655360
Sparse Core Ops, SparseCore 0:
  13.1 146.6 reduce-scatter.5
  163.1 75.7 all-gather.2
  273.6 141.1 reduce-scatter.7
  417.9 50.2 all-reduce.4
  471.5 187.7 all-reduce.6
  822.8 73.6 all-gather.4
  900.3 22.7 reduce-scatter.9
